TPU v7x, 1024 devices: a whole 8x8x8 slice. The times are simulated.
1024 devices in a mesh: ctx: 64 (over z, x), tp: 16 (over y, core).
Axes of the slice: x: 8, y: 8, z: 8, core: 2. Of those that a mesh axis runs over, the one named last changes fastest.
Arguments:
- projected: bfloat16 [3, 16384, 8192], P(None, 'ctx', 'tp'), may hold values from -6 to 6
- short_filter: float32 [3, 7, 512], P(None, None, 'tp'), may hold values from -2 to 2
- long_filter: bfloat16 [128, 512], P(None, 'tp'), may hold values from -0.5 to 0.5
- out_weight: bfloat16 [8192, 8192], P('tp'), may hold values from -0.0625 to 0.0625
- out_grad: bfloat16 [16384, 8192], P(('ctx', 'tp')), may hold values from -6 to 6
Outputs:
- projected_grad: bfloat16 [3, 16384, 8192], P(None, 'ctx', 'tp')
- short_grad: float32 [3, 7, 512], P(None, None, 'tp')
- long_grad: float32 [128, 512], P(None, 'tp')
All inputs are finite; a program needn't handle non-finite values.
Results may differ from a plain program's by a relative error of at most 0.013.
Values may be sent and summed in bfloat16 or wider, within the bound.
A program may use at most 64 MiB of HBM per device.

v0:
```python
import math

import jax
import jax.numpy as jnp
from jax import lax
from jax.sharding import PartitionSpec as P


def passed_along(value, axis, steps):
    count = lax.axis_size(axis)
    first, last = (max(0, -steps), min(count, count - steps))
    return lax.ppermute(value, axis, [(source, source + steps) for source in range(first, last)])


def filter_matrix(taps, forward):
    length = taps.shape[0]
    lines = jnp.arange(length, dtype=jnp.int32)[:, None]
    places = jnp.arange(2 * length - 1, dtype=jnp.int32)[None, :]
    offset = lines + length - 1 - places if forward else places - lines
    valid = (offset >= 0) & (offset < length)
    index = jnp.clip(offset, 0, length - 1)
    return jnp.where(valid[None], taps.T[:, index], jnp.zeros((), taps.dtype))


def long_apply(extended, matrix):
    length = matrix.shape[1]
    groups = matrix.shape[0]
    channels = extended.shape[1]
    count = extended.shape[0] - (length - 1)
    columns = extended.T

    def one_block(block):
        window = lax.dynamic_slice_in_dim(columns, block * length, 2 * length - 1, 1)
        window = window.reshape(groups, channels // groups, 2 * length - 1)
        result = jnp.einsum("gtj,gcj->gct", matrix, window, preferred_element_type=jnp.float32)
        return result.reshape(channels, length)

    blocks = jnp.arange(count // length, dtype=jnp.int32)
    stacked = lax.map(one_block, blocks)
    return jnp.transpose(stacked, (1, 0, 2)).reshape(channels, count).T


def long_filter_grad(grads, extended, groups):
    count = grads.shape[0]
    channels = grads.shape[1]
    length = extended.shape[0] - count + 1
    grad_cols = grads.T
    ext_cols = extended.T

    def one_block(block):
        window = lax.dynamic_slice_in_dim(ext_cols, block * length, 2 * length - 1, 1)
        window = window.reshape(groups, channels // groups, 2 * length - 1)
        part = lax.dynamic_slice_in_dim(grad_cols, block * length, length, 1)
        part = part.reshape(groups, channels // groups, length)
        table = jnp.einsum("gct,gcj->gtj", part, window, preferred_element_type=jnp.float32)
        flat = table.reshape(groups, length * (2 * length - 1))
        flat = jnp.pad(flat, ((0, 0), (0, length))).reshape(groups, length, 2 * length)
        return jnp.sum(flat[:, :, :length], axis=1)

    blocks = jnp.arange(count // length, dtype=jnp.int32)
    sums = jnp.sum(lax.map(one_block, blocks), axis=0)
    return sums[:, ::-1].T


def short_apply(extended, taps_ch):
    size = taps_ch.shape[1]
    count = extended.shape[1] - (size - 1)
    total = jnp.zeros((3, count, extended.shape[2]), jnp.float32)
    for tap in range(size):
        start = size - 1 - tap
        total = total + taps_ch[:, tap, None, :] * extended[:, start : start + count].astype(
            jnp.float32
        )
    return total


def short_back(extended, taps_ch):
    size = taps_ch.shape[1]
    count = extended.shape[1] - (size - 1)
    total = jnp.zeros((3, count, extended.shape[2]), jnp.float32)
    for tap in range(size):
        total = total + taps_ch[:, tap, None, :] * extended[:, tap : tap + count].astype(
            jnp.float32
        )
    return total


def short_filter_grad(grads, extended, groups):
    count = grads.shape[1]
    size = extended.shape[1] - count + 1
    channels = grads.shape[2]
    grads_wide = grads.astype(jnp.float32)
    pieces = []
    for tap in range(size):
        start = size - 1 - tap
        pieces.append(
            jnp.sum(grads_wide * extended[:, start : start + count].astype(jnp.float32), axis=1)
        )
    stacked = jnp.stack(pieces, axis=1)
    return jnp.sum(stacked.reshape(3, size, groups, channels // groups), axis=3)


def key_value(mixed):
    return (mixed[1].astype(jnp.float32) * mixed[2].astype(jnp.float32)).astype(jnp.bfloat16)


def per_device(projected, short_filter, long_filter, out_weight, out_grad):
    count = projected.shape[1]
    channels = projected.shape[2]
    taps_long = long_filter.shape[0]
    taps_short = short_filter.shape[1]
    groups = long_filter.shape[1]
    per_group = channels // groups
    short_ch = jnp.repeat(short_filter, per_group, axis=2)
    forward_mat = filter_matrix(long_filter, True)
    backward_mat = filter_matrix(long_filter, False)
    reach = taps_long + taps_short - 2
    received = passed_along(projected[:, count - reach :], "ctx", 1)
    widened = jnp.concatenate([received, projected], 1)
    mixed_all = short_apply(widened, short_ch).astype(jnp.bfloat16)
    padded = key_value(mixed_all)
    mixed = mixed_all[:, taps_long - 1 :]
    extended = widened[:, taps_long - 1 :]
    query, key_part, value = (mixed[0], mixed[1], mixed[2])
    response = long_apply(padded, forward_mat)
    out_branch = lax.dot_general(
        lax.all_gather(out_grad, "tp", axis=0, tiled=True),
        out_weight,
        (((1,), (1,)), ((), ())),
        preferred_element_type=jnp.float32,
    ).astype(jnp.bfloat16)
    branch_wide = out_branch.astype(jnp.float32)
    grad_query = (branch_wide * response).astype(jnp.bfloat16)
    grad_resp = (branch_wide * query.astype(jnp.float32)).astype(jnp.bfloat16)
    head_prod = long_apply(grad_resp[: 2 * taps_long - 1], backward_mat)[: taps_short - 1]
    head_prod = head_prod.astype(jnp.bfloat16).astype(jnp.float32)
    head_mixed = jnp.stack(
        [
            grad_query[: taps_short - 1],
            (head_prod * value[: taps_short - 1].astype(jnp.float32)).astype(jnp.bfloat16),
            (head_prod * key_part[: taps_short - 1].astype(jnp.float32)).astype(jnp.bfloat16),
        ],
        axis=0,
    )
    next_resp, next_mixed = passed_along((grad_resp[: taps_long - 1], head_mixed), "ctx", -1)
    grad_prod = long_apply(jnp.concatenate([grad_resp, next_resp], 0), backward_mat).astype(
        jnp.bfloat16
    )
    prod_wide = grad_prod.astype(jnp.float32)
    grad_key = (prod_wide * value.astype(jnp.float32)).astype(jnp.bfloat16)
    grad_value = (prod_wide * key_part.astype(jnp.float32)).astype(jnp.bfloat16)
    grad_mixed = jnp.stack([grad_query, grad_key, grad_value], axis=0)
    projected_grad = short_back(jnp.concatenate([grad_mixed, next_mixed], 1), short_ch).astype(
        jnp.bfloat16
    )
    long_part = long_filter_grad(grad_resp, padded, groups)
    short_part = short_filter_grad(grad_mixed, extended, groups)
    short_sum, long_sum = lax.psum((short_part, long_part), "ctx")
    scale = 1.0 / math.sqrt(lax.axis_size("ctx") * count * per_group)
    return (projected_grad, short_sum * scale, long_sum * scale)


def solution(mesh):
    placed = (
        P(None, "ctx", "tp"),
        P(None, None, "tp"),
        P(None, "tp"),
        P("tp", None),
        P(("ctx", "tp"), None),
    )
    return jax.shard_map(
        per_device,
        mesh=mesh,
        in_specs=placed,
        out_specs=(P(None, "ctx", "tp"), P(None, None, "tp"), P(None, "tp")),
        check_vma=False,
    )
```

profile of v0, /device:TPU:112, one launch (start us, length us, event | category | flops | bytes accessed | tf_op | source)
XLA Modules:
  0.0 562.6 jit_solution(1069082375630771817)
XLA Ops:
  7.9 1.9 slice.146
  9.8 3.4 collective-permute-start
  14.9 66.3 %gather_fusion = bf16[32640,32]{1,0:T(8,128)(2,1)} fusion(bf16[32,128]{0,1:T(8,128)(2,1)S(1)} %bitcast.172, s32[32768]{0:T(1024)S(1)} %pad_clamp_fusion.1), kind=kCustom, calls=%fused_computation | custom fusion | bytes 4308480 | tf_op jit(solution)/shard_map/gather | solution.py:22
  81.2 7.9 %copy.32 = bf16[32640,32]{0,1:T(8,128)(2,1)} copy(bf16[32640,32]{1,0:T(8,128)(2,1)} %gather_fusion) | data formatting | bytes 4177920 | tf_op jit(solution)/shard_map/gather | solution.py:22
  89.1 9.0 %reshape.222 = bf16[128,255,32]{1,0,2:T(8,128)(2,1)} reshape(bf16[32640,32]{0,1:T(8,128)(2,1)} %copy.32) | data formatting | bytes 4177920 | tf_op jit(solution)/shard_map/gather | solution.py:22
  98.5 66.3 %gather_fusion.1 = bf16[32640,32]{1,0:T(8,128)(2,1)} fusion(bf16[32,128]{0,1:T(8,128)(2,1)S(1)} %bitcast.173, s32[32768]{0:T(1024)S(1)} %pad_clamp_fusion), kind=kCustom, calls=%fused_computation.1 | custom fusion | bytes 4308480 | tf_op jit(solution)/shard_map/gather | solution.py:22
  164.8 7.9 %copy.35 = bf16[32640,32]{0,1:T(8,128)(2,1)} copy(bf16[32640,32]{1,0:T(8,128)(2,1)} %gather_fusion.1) | data formatting | bytes 4177920 | tf_op jit(solution)/shard_map/gather | solution.py:22
  172.7 9.2 %reshape.230 = bf16[128,255,32]{1,0,2:T(8,128)(2,1)} reshape(bf16[32640,32]{0,1:T(8,128)(2,1)} %copy.35) | data formatting | bytes 4177920 | tf_op jit(solution)/shard_map/gather | solution.py:22
  186.4 2.3 add_convert_fusion
  190.2 7.4 %while.39 = (s32[]{:T(128)}, f32[2,512,128]{2,1,0:T(8,128)S(1)}, s32[2]{0:T(128)S(1)}, bf16[512,383]{1,0:T(8,128)(2,1)S(1)}, bf16[32,128,255]{2,1,0:T(8,128)(2,1)}, /*index=5*/s32[1]{0:T(128)}) while((s32[]{:T(128)}, f32[2,512,128]{2,1,0:T(8,128)S(1)}, s32[2]{0:T(128)S(1)}, bf16[512,383]{1,0:T(8,128)(2,1)S(1)}, ...), condition=%wide.region_1.2_spmd.clone, body=%wide.region_0.1_spmd.sunk.clone | while | flops 33423364 | bytes 3658895 | solution.py:39
  191.6 2.2 fusion.76
  195.3 2.2 fusion.76
  198.6 7.1 %fusion.30 = (bf16[256,512]{1,0:T(8,128)(2,1)S(1)}, bf16[256,512]{1,0:T(8,128)(2,1)S(1)}) fusion(f32[512,2,128]{0,2,1:T(8,128)} %copy.34, bf16[3,383,512]{2,1,0:T(8,128)(2,1)} %copy-done.2, bf16[256,8192]{1,0:T(8,128)(2,1)} %all-gather.2.cloned.1.call-done, bf16[512,8192]{1,0:T(8,128)(2,1)} %param.14), kind=kOutput, calls=%fused_computation.85 | convolution fusion | flops 2148401152 | bytes 13893632 | tf_op jit(solution)/shard_map/dot_general | solution.py:126
  211.2 29.5 %while.41 = (s32[]{:T(128)}, f32[2,32,128]{2,1,0:T(8,128)}, s32[2]{0:T(128)S(1)}, bf16[512,256]{0,1:T(8,128)(2,1)S(1)}, bf16[512,383]{1,0:T(8,128)(2,1)S(1)}, /*index=5*/s32[1]{0:T(128)}) while((s32[]{:T(128)}, f32[2,32,128]{2,1,0:T(8,128)}, s32[2]{0:T(128)S(1)}, bf16[512,256]{0,1:T(8,128)(2,1)S(1)}, ...), condition=%wide.region_15.16_spmd.clone, body=%wide.region_13.15_spmd.sunk.clone | while | flops 33943560 | bytes 33141992 | solution.py:61
  213.0 2.7 fusion.82
  215.7 5.2 reshape.237
  220.9 2.5 pad.189
  227.6 2.7 fusion.82
  230.3 5.2 reshape.237
  235.6 2.5 pad.189
  243.6 7.4 %while.40 = (s32[]{:T(128)}, bf16[2,512,128]{2,1,0:T(8,128)(2,1)}, s32[2]{0:T(128)}, bf16[512,383]{0,1:T(8,128)(2,1)S(1)}, bf16[32,128,255]{2,1,0:T(8,128)(2,1)S(1)}, /*index=5*/s32[1]{0:T(128)}) while((s32[]{:T(128)}, bf16[2,512,128]{2,1,0:T(8,128)(2,1)}, s32[2]{0:T(128)}, bf16[512,383]{0,1:T(8,128)(2,1)S(1)}, ...), condition=%wide.region_3.4_spmd.clone, body=%wide.region_2.3_spmd.sunk.clone | while | flops 33423364 | bytes 5885127 | solution.py:39
  254.4 2.3 fusion.6
  256.7 1.6 fusion.12
  259.2 295.3 %all-reduce.1 = (f32[3,7,32]{2,0,1:T(4,128)S(1)}, f32[128,32]{0,1:T(8,128)S(1)}) all-reduce(f32[3,7,32]{2,0,1:T(4,128)S(1)} %reduce_sum.100, f32[128,32]{0,1:T(8,128)S(1)} %bitcast.199), channel_id=1, replica_groups=mesh['ctx'=64,'tp'=16] {'ctx'}, use_global_device_ids=true, to_apply=%region_12.13 | all-reduce | flops 4768 | bytes 38144 | tf_op jit(solution)/shard_map/psum | solution.py:158
  (153 shorter events, 38.0 us)
Async XLA Ops:
  7.2 7.1 %copy-start.22 = (bf16[128,32]{0,1:T(8,128)(2,1)S(1)}, bf16[128,32]{0,1:T(8,128)(2,1)}, u32[]{:S(2)}) copy-start(bf16[128,32]{0,1:T(8,128)(2,1)} %param.13) | copy-start | bytes 24580
  7.2 191.4 %all-gather.2.cloned.1.call-start = ((), (), s32[]{:S(2)}) async-start(), calls=%async_computation | async-start | bytes 4456448 | tf_op jit(solution)/shard_map/all_gather | solution.py:127
  9.8 175.5 %collective-permute-start = (bf16[3,133,512]{2,1,0:T(8,128)(2,1)}, bf16[3,133,512]{2,1,0:T(8,128)(2,1)S(1)}, u32[]{:S(2)}, u32[]{:S(2)}) collective-permute-start(bf16[3,133,512]{2,1,0:T(8,128)(2,1)} %slice.146), channel_id=1, source_target_pairs={{0,16},{16,32},{32,48},{48,64},{64,80},{80,96},{96,112},{112,128},... | collective-permute-start | bytes 1225736 | tf_op jit(solution)/shard_map/ppermute | solution.py:12
  172.7 10.1 %copy-start = (bf16[128,255,32]{1,0,2:T(8,128)(2,1)S(1)}, bf16[128,255,32]{1,0,2:T(8,128)(2,1)}, u32[]{:S(2)}) copy-start(bf16[128,255,32]{1,0,2:T(8,128)(2,1)} %reshape.222) | copy-start | bytes 6266884
  182.6 2.7 copy-start.9
  182.6 2.7 copy-start.11
  182.6 2.7 copy-start.13
  182.7 2.7 copy-start.15
  182.7 2.7 copy-start.17
  182.8 2.3 copy-start.1
  185.2 1.3 copy-start.3
  185.3 3.4 copy-start.5
  188.8 1.1 copy-start.2
  208.6 44.8 %collective-permute-start.2 = (bf16[3,6,512]{2,1,0:T(8,128)(2,1)}, bf16[3,6,512]{2,1,0:T(8,128)(2,1)}, u32[]{:S(2)}, u32[]{:S(2)}) collective-permute-start(bf16[3,6,512]{2,1,0:T(8,128)(2,1)} %pad_maximum_fusion.3), channel_id=1, source_target_pairs={{16,0},{32,16},{48,32},{64,48},{80,64},{96,80},{112,96},{128,112},... | collective-permute-start | bytes 55304 | tf_op jit(solution)/shard_map/ppermute | solution.py:12
  209.9 32.2 %collective-permute-start.1 = (bf16[127,512]{1,0:T(8,128)(2,1)}, bf16[127,512]{1,0:T(8,128)(2,1)}, u32[]{:S(2)}, u32[]{:S(2)}) collective-permute-start(bf16[127,512]{1,0:T(8,128)(2,1)} %slice.212), channel_id=1, source_target_pairs={{16,0},{32,16},{48,32},{64,48},{80,64},{96,80},{112,96},{128,112},... | collective-permute-start | bytes 390152 | tf_op jit(solution)/shard_map/ppermute | solution.py:12
  245.6 1.0 copy-start.7
  252.2 2.1 copy-start.10
  252.2 2.1 copy-start.12
  252.2 2.1 copy-start.14
  252.2 2.1 copy-start.16
  252.2 2.1 copy-start.18
  254.3 2.3 copy-start.4
  254.4 2.3 copy-start.6
  256.6 2.5 copy-start.19
  (7 other events, 5.2 us)
Sparse Core Ops, SparseCore 0:
  10.7 56.7 all-gather.1
where the time goes:
time: 564 us; the launch traced here: 563 us
  blocking collectives  295 us (52%)
  local copies, waits for them, and re-layouts  207 us (37%)
  matrix products  18.8 us (3%)
  other arithmetic  16.2 us (3%)
  between operations  14.6 us (3%)
  starting transfers between devices  6.02 us (1%)
    psum x1, blocking collectives, per_device(): short_sum, long_sum = lax.psum((short_part, long_part), 'ctx')  295 us
    gather x6, local copies, waits for them, and re-layouts, filter_matrix(): return jnp.where(valid[None], taps.T[:, index], jnp.zeros((), taps.dtype))  167 us
  transfers between devices with their start and end apart: 4, of which 0 were waited for; matrix products, arithmetic and copies ran while one was open for 39% of the time, Pallas kernels for 0%

commit v1 on v0

v1 whole, which is shorter than its diff:
```python
import functools
import math

import jax
import jax.numpy as jnp
from jax import lax
from jax.experimental import pallas as pl
from jax.experimental.pallas import tpu as pltpu
from jax.sharding import PartitionSpec as P

MESH = pl.DeviceIdType.MESH
BF = jnp.bfloat16
F32 = jnp.float32
HALO = 144
LB = 128
NT = (((1,), (1,)), ((), ()))
TN = (((0,), (0,)), ((), ()))
HI = lax.Precision.HIGHEST


def one_hot(shape, test):
    rows = lax.broadcasted_iota(jnp.int32, shape, 0)
    cols = lax.broadcasted_iota(jnp.int32, shape, 1)
    return jnp.where(test(rows, cols), 1.0, 0.0)


def kernel(
    dims,
    scale,
    proj_hbm,
    sf_ref,
    lf_ref,
    w_hbm,
    og_hbm,
    pg_hbm,
    sg_ref,
    lg_ref,
    gath,
    wv,
    pw,
    pf,
    mixed,
    prod,
    resp,
    fmat,
    bmat,
    taps_f,
    taps_b,
    taps_ch,
    acc,
    grb,
    nxt,
    gm,
    head_out,
    head_in,
    gp1,
    lacc,
    sgc,
    xbuf,
    zbuf,
    pgv,
    local_sem,
    ring_send,
    ring_recv,
    sib_send,
    sib_recv,
    halo_send,
    halo_recv,
    x_send,
    x_recv,
    z_send,
    z_recv,
    out_sem,
):
    nx, nz, ny = dims
    n_ctx = nx * nz
    i = lax.axis_index("ctx")
    k = lax.axis_index("tp")
    x, z = lax.rem(i, nx), i // nx
    y, core = k // 2, lax.rem(k, 2)
    count = proj_hbm.shape[1]
    chan = proj_hbm.shape[2]
    model = w_hbm.shape[1]
    short = sf_ref.shape[1]
    long = lf_ref.shape[0]
    groups = lf_ref.shape[1]
    per_group = chan // groups
    lanes_n = chan // LB
    in_block = LB // per_group
    rows_chip = 2 * og_hbm.shape[0]
    half = model // 2

    right = lax.rem(y + 1, ny) * 2 + core
    left = lax.rem(y + ny - 1, ny) * 2 + core
    sibling = y * 2 + 1 - core
    following = lax.rem(i + 1, n_ctx)
    previous = lax.rem(i + n_ctx - 1, n_ctx)
    x_peers = [z * nx + lax.rem(x + d, nx) for d in range(1, nx)]
    z_peers = [lax.rem(z + d, nz) * nx + x for d in range(1, nz)]

    barrier = pltpu.get_barrier_semaphore()
    tp_greet = [right, left, sibling]
    ctx_greet = [following, previous] + x_peers + z_peers
    for other in tp_greet:
        pl.semaphore_signal(barrier, inc=1, device_id={"tp": other}, device_id_type=MESH)
    for other in ctx_greet:
        pl.semaphore_signal(barrier, inc=1, device_id={"ctx": other}, device_id_type=MESH)

    og_copy = pltpu.make_async_copy(og_hbm, gath.at[k], local_sem.at[0])
    og_copy.start()
    proj_copy = pltpu.make_async_copy(proj_hbm, pw.at[:, pl.ds(HALO, count), :], local_sem.at[1])
    proj_copy.start()
    w_copy = pltpu.make_async_copy(w_hbm, wv, local_sem.at[2])
    w_copy.start()
    og_copy.wait()
    proj_copy.wait()
    pl.semaphore_wait(barrier, len(tp_greet) + len(ctx_greet))

    steps = ny // 2

    def chunks(direction, step):
        return (0, 1) if step < steps else (direction,)

    def chip_at(direction, distance):
        if direction == 0:
            return lax.rem(y + ny - distance, ny)
        return lax.rem(y + distance, ny)

    def part(direction, distance, chunk):
        block = chip_at(direction, distance) * 2 + core
        return gath.at[block, :, pl.ds(chunk * half, half)]

    def ring(direction, step, chunk):
        ref = part(direction, step - 1, chunk)
        return pltpu.make_async_remote_copy(
            src_ref=ref,
            dst_ref=ref,
            send_sem=ring_send.at[direction, step - 1, chunk],
            recv_sem=ring_recv.at[direction, step - 1, chunk],
            device_id={"tp": right if direction == 0 else left},
            device_id_type=MESH,
        )

    def ring_arrival(direction, step, chunk):
        ref = part(direction, step, chunk)
        return pltpu.make_async_remote_copy(
            src_ref=ref,
            dst_ref=ref,
            send_sem=ring_send.at[direction, step - 1, chunk],
            recv_sem=ring_recv.at[direction, step - 1, chunk],
            device_id={"tp": right if direction == 0 else left},
            device_id_type=MESH,
        )

    def across(direction, step, chunk, own):
        block = chip_at(direction, step) * 2 + (core if own else 1 - core)
        ref = gath.at[block, :, pl.ds(chunk * half, half)]
        return pltpu.make_async_remote_copy(
            src_ref=ref,
            dst_ref=ref,
            send_sem=sib_send.at[direction, step, chunk],
            recv_sem=sib_recv.at[direction, step, chunk],
            device_id={"tp": sibling},
            device_id_type=MESH,
        )

    for chunk in range(2):
        for direction in range(2):
            if chunk in chunks(direction, 1):
                ring(direction, 1, chunk).start()
    halo = pltpu.make_async_remote_copy(
        src_ref=pw.at[:, pl.ds(count, HALO), :],
        dst_ref=pw.at[:, pl.ds(0, HALO), :],
        send_sem=halo_send.at[0],
        recv_sem=halo_recv.at[0],
        device_id={"ctx": following},
        device_id_type=MESH,
    )
    halo.start()
    for chunk in range(2):
        across(0, 0, chunk, True).start()

    def service(step, chunk):
        for direction in range(2):
            if chunk in chunks(direction, step):
                ring_arrival(direction, step, chunk).wait_recv()
                if step < steps and chunk in chunks(direction, step + 1):
                    ring(direction, step + 1, chunk).start()
                across(direction, step, chunk, True).start()

    def across_arrivals(step):
        for direction in range(2 if step > 0 else 1):
            for chunk in chunks(direction, step):
                across(direction, step, chunk, False).wait_recv()

    def build_taps():
        spread = one_hot((groups, chan), lambda r, c: c // per_group == r)
        for j in range(3):
            taps_ch[j, 0:short, :] = jnp.dot(
                sf_ref[j], spread, precision=HI, preferred_element_type=F32
            )
        lf = lf_ref[...].astype(F32)
        taps_f[...] = lax.dot_general(
            lf,
            one_hot((long, 2 * long), lambda r, c: c == long - r),
            TN,
            preferred_element_type=F32,
        )
        taps_b[...] = lax.dot_general(
            lf, one_hot((long, 2 * long), lambda r, c: c == r), TN, preferred_element_type=F32
        )

    def build_matrix(taps, matrix, start, stop):
        def body(g, carry):
            row = jnp.broadcast_to(taps[pl.ds(g, 1), :], (long, 2 * long))
            turned = pltpu.roll(row, 0, 1, stride=1, stride_axis=0)
            matrix[pl.ds(pl.multiple_of(g * long, long), long), :] = turned.astype(BF)
            return carry

        lax.fori_loop(start, stop, body, 0)

    lane_group = lax.broadcasted_iota(jnp.int32, (long, LB), 1) // per_group

    def pick(result, b):
        total = jnp.zeros((long, LB), F32)
        for g in range(in_block):
            piece = result[g * long : (g + 1) * long, b * LB : (b + 1) * LB]
            total = jnp.where(lane_group == g, piece, total)
        return total

    def lane_slice(lb):
        return pl.ds(pl.multiple_of(lb * LB, LB), LB)

    def group_rows(lb):
        return pl.ds(pl.multiple_of(lb * in_block * long, in_block * long), in_block * long)

    def widen():
        def body(j, carry):
            pf[j, HALO : HALO + count, :] = pw[j, HALO : HALO + count, :].astype(F32)
            edge = pw[j, 0:HALO, :].astype(F32)
            pf[j, 0:HALO, :] = jnp.where(i == 0, 0.0, edge)
            return carry

        lax.fori_loop(0, 3, body, 0)

    base = HALO - long

    def short_forward():
        def body(step, carry):
            j, lb = step // lanes_n, lax.rem(step, lanes_n)
            ls = lane_slice(lb)
            for blk in range(3):
                total = jnp.zeros((long, LB), F32)
                for s in range(short):
                    first = base + blk * long - s
                    total = total + taps_ch[j, s : s + 1, ls] * pf[j, first : first + long, ls]
                mixed[j, blk * long : (blk + 1) * long, ls] = total.astype(BF)
            return carry

        lax.fori_loop(0, 3 * lanes_n, body, 0)

    def long_forward():
        def body(lb, carry):
            ls = lane_slice(lb)
            value = mixed[1, :, ls].astype(F32) * mixed[2, :, ls].astype(F32)
            prod[:, ls] = value.astype(BF)
            window = jnp.concatenate([prod[0 : 2 * long, ls], prod[long : 3 * long, ls]], axis=1)
            result = jnp.dot(fmat[group_rows(lb), :], window, preferred_element_type=F32)
            for b in range(2):
                resp[b * long : (b + 1) * long, ls] = pick(result, b)
            return carry

        lax.fori_loop(0, lanes_n, body, 0)

    kc = min(1024, model)

    def project(chips):
        def body(c, carry):
            cols = pl.ds(pl.multiple_of(c * kc, kc), kc)
            xs = [gath[pl.ds(2 * chip, 2), :, cols].reshape(rows_chip, kc) for chip in chips]
            lhs = jnp.concatenate(xs, axis=0) if len(xs) > 1 else xs[0]
            return carry + lax.dot_general(lhs, wv[:, cols], NT, preferred_element_type=F32)

        zero = jnp.zeros((rows_chip * len(chips), chan), F32)
        total = lax.fori_loop(0, model // kc, body, zero)
        for q, chip in enumerate(chips):
            rows = pl.ds(pl.multiple_of(chip * rows_chip, rows_chip), rows_chip)
            acc[rows, :] = total[q * rows_chip : (q + 1) * rows_chip].astype(BF)

    def branch(chips):
        for chip in chips:
            start = chip * rows_chip
            rows = pl.ds(pl.multiple_of(start, rows_chip), rows_chip)
            own = pl.ds(pl.multiple_of(start + long, rows_chip), rows_chip)
            ob = acc[rows, :].astype(F32)
            gm[0, own, :] = (ob * resp[rows, :]).astype(BF).astype(F32)
            grb[own, :] = (ob * mixed[0, own, :].astype(F32)).astype(BF)

    build_taps()
    build_matrix(taps_f, fmat, 0, groups)
    grb[0:long, :] = jnp.zeros((long, chan), BF)
    grb[long + count :, :] = jnp.zeros((long, chan), BF)
    gm[0, 0:long, :] = jnp.zeros((long, chan), F32)
    for j in range(3):
        sgc[j, :, :] = jnp.zeros((8, chan), F32)

    if steps > 1:
        service(1, 0)
    build_matrix(taps_b, bmat, 0, groups)
    w_copy.wait()
    if steps > 1:
        service(1, 1)
        across_arrivals(0)
        across_arrivals(1)
        near = [y, chip_at(0, 1), chip_at(1, 1)]
    else:
        across_arrivals(0)
        near = [y]
    project(near)
    halo.wait_recv()
    if steps > 2:
        service(2, 0)
    widen()
    short_forward()
    if steps > 2:
        service(2, 1)
    long_forward()
    branch(near)
    for step in range(3, steps):
        service(step, 0)
        service(step, 1)
    middle = []
    for step in range(2, steps):
        across_arrivals(step)
        middle += [chip_at(0, step), chip_at(1, step)]
    if middle:
        project(middle)
        branch(middle)
    service(steps, 0)
    service(steps, 1)
    across_arrivals(steps)
    far = [chip_at(0, steps)]
    project(far)
    branch(far)

    back = pltpu.make_async_remote_copy(
        src_ref=grb.at[pl.ds(long, long), :],
        dst_ref=nxt,
        send_sem=halo_send.at[1],
        recv_sem=halo_recv.at[1],
        device_id={"ctx": previous},
        device_id_type=MESH,
    )

    def long_backward():
        def body(lb, carry):
            ls = lane_slice(lb)
            window = jnp.concatenate(
                [grb[b * long : (b + 2) * long, ls] for b in range(3)], axis=1
            )
            result = jnp.dot(bmat[group_rows(lb), :], window, preferred_element_type=F32)
            for b in range(3):
                rows = slice(b * long, (b + 1) * long)
                grad = pick(result, b)
                if b == 2:
                    gp1[:, ls] = grad
                grad = grad.astype(BF).astype(F32)
                gm[1, rows, ls] = (grad * mixed[2, rows, ls].astype(F32)).astype(BF).astype(F32)
                gm[2, rows, ls] = (grad * mixed[1, rows, ls].astype(F32)).astype(BF).astype(F32)
            return carry

        lax.fori_loop(0, lanes_n, body, 0)

    def long_taps():
        flip = one_hot((long, long), lambda r, c: r + c == long - 1).astype(BF)
        wide_group = lax.broadcasted_iota(jnp.int32, (long, 2 * LB), 1) % LB // per_group

        def body(lb, carry):
            ls = lane_slice(lb)
            grads = jnp.concatenate(
                [grb[long : 2 * long, ls], grb[2 * long : 3 * long, ls]], axis=1
            )
            grads = jnp.dot(flip, grads, preferred_element_type=F32).astype(BF)
            window = jnp.concatenate([prod[0 : 2 * long, ls], prod[long : 3 * long, ls]], axis=1)
            only = [
                jnp.where(wide_group == g, grads, jnp.zeros_like(grads)) for g in range(in_block)
            ]
            table = lax.dot_general(
                jnp.concatenate(only, axis=0), window, NT, preferred_element_type=F32
            )
            sums = []
            for g in range(in_block):
                piece = table[g * long : (g + 1) * long]
                turned = pltpu.roll(piece, 0, 1, stride=1, stride_axis=0)
                sums.append(jnp.sum(turned, axis=0, keepdims=True))
            rows = pl.ds(pl.multiple_of(lb * in_block, in_block), in_block)
            lacc[rows, :] = jnp.concatenate(sums, axis=0)
            return carry

        lax.fori_loop(0, lanes_n, body, 0)

    def short_taps():
        def body(step, carry):
            j, lb = step // lanes_n, lax.rem(step, lanes_n)
            ls = lane_slice(lb)
            for s in range(short):
                total = jnp.zeros((1, LB), F32)
                for blk in range(3):
                    first = base + blk * long - s
                    both = gm[j, blk * long : (blk + 1) * long, ls] * pf[j, first : first + long, ls]
                    total = total + jnp.sum(both, axis=0, keepdims=True)
                sgc[j, s : s + 1, ls] = total
            return carry

        lax.fori_loop(0, 3 * lanes_n, body, 0)

    back.start()
    long_backward()
    head_out[...] = gm[:, long : long + 16, :].astype(BF)
    long_taps()
    head = pltpu.make_async_remote_copy(
        src_ref=head_out,
        dst_ref=head_in,
        send_sem=halo_send.at[2],
        recv_sem=halo_recv.at[2],
        device_id={"ctx": previous},
        device_id_type=MESH,
    )
    head.start()
    short_taps()

    xbuf[x, 0:groups, :] = lacc[:, long : 2 * long]
    total = jnp.zeros((8, LB), F32)
    for j in range(3):
        place = one_hot((chan, LB), lambda r, c: c - groups * j == r // per_group)
        total = total + jnp.dot(sgc[j], place, precision=HI, preferred_element_type=F32)
    xbuf[x, groups : groups + 8, :] = total

    def exchange(buf, me, size, peers, send, recv):
        def copy(slot, d):
            return pltpu.make_async_remote_copy(
                src_ref=buf.at[slot],
                dst_ref=buf.at[slot],
                send_sem=send.at[d - 1],
                recv_sem=recv.at[slot],
                device_id={"ctx": peers[d - 1]},
                device_id_type=MESH,
            )

        return [copy(me, d) for d in range(1, size)], [
            copy(lax.rem(me + d, size), d) for d in range(1, size)
        ]

    order = lambda size: sorted(range(size - 1), key=lambda d: -min(d + 1, size - d - 1))
    x_out, x_in = exchange(xbuf, x, nx, x_peers, x_send, x_recv)
    for d in order(nx):
        x_out[d].start()

    back.wait_recv()
    last = i == n_ctx - 1

    def finish_backward():
        def body(lb, carry):
            ls = lane_slice(lb)
            window = nxt[:, ls]
            window = jnp.where(last, jnp.zeros_like(window), window)
            result = jnp.dot(
                bmat[group_rows(lb), long : 2 * long], window, preferred_element_type=F32
            )
            rows = slice(2 * long, 3 * long)
            grad = (gp1[:, ls] + pick(result, 0)).astype(BF).astype(F32)
            gm[1, rows, ls] = (grad * mixed[2, rows, ls].astype(F32)).astype(BF).astype(F32)
            gm[2, rows, ls] = (grad * mixed[1, rows, ls].astype(F32)).astype(BF).astype(F32)
            return carry

        lax.fori_loop(0, lanes_n, body, 0)

    finish_backward()
    head.wait_recv()
    ahead = head_in[...].astype(F32)
    gm[:, long + count : long + count + 16, :] = jnp.where(last, 0.0, ahead)

    def short_backward():
        def body(step, carry):
            j, lb = step // lanes_n, lax.rem(step, lanes_n)
            ls = lane_slice(lb)
            for blk in range(2):
                total = jnp.zeros((long, LB), F32)
                for s in range(short):
                    first = (blk + 1) * long + s
                    total = total + taps_ch[j, s : s + 1, ls] * gm[j, first : first + long, ls]
                pgv[j, blk * long : (blk + 1) * long, ls] = total.astype(BF)
            return carry

        lax.fori_loop(0, 3 * lanes_n, body, 0)

    for d in range(nx - 1):
        x_in[d].wait_recv()
    total = xbuf[0]
    for d in range(1, nx):
        total = total + xbuf[d]
    zbuf[z, :, :] = total
    z_out, z_in = exchange(zbuf, z, nz, z_peers, z_send, z_recv)
    short_backward()
    for d in order(nz):
        z_out[d].start()
    out_copy = pltpu.make_async_copy(pgv, pg_hbm, out_sem)
    out_copy.start()
    for d in range(nz - 1):
        z_in[d].wait_recv()
    total = zbuf[0]
    for d in range(1, nz):
        total = total + zbuf[d]
    total = total * scale
    lg_ref[...] = lax.dot_general(
        one_hot((long, long), lambda r, c: r + c == long - 1),
        total[0:groups],
        NT,
        precision=HI,
        preferred_element_type=F32,
    )
    for j in range(3):
        place = one_hot((LB, groups), lambda r, c: r - groups * j == c)
        sums = jnp.dot(total[groups : groups + 8], place, precision=HI, preferred_element_type=F32)
        sg_ref[j] = sums[0:short]

    for step in range(1, steps + 1):
        for direction in range(2):
            for chunk in chunks(direction, step):
                ring(direction, step, chunk).wait_send()
                across(direction, step, chunk, True).wait_send()
    for chunk in range(2):
        across(0, 0, chunk, True).wait_send()
    halo.wait_send()
    back.wait_send()
    head.wait_send()
    for copy in x_out + z_out:
        copy.wait_send()
    out_copy.wait()


def solution(mesh):
    n_ctx, n_tp = mesh.shape["ctx"], mesh.shape["tp"]
    nx = math.isqrt(n_ctx)
    nx = nx if nx * nx == n_ctx else n_ctx
    dims = (nx, n_ctx // nx, n_tp // 2)

    def step(projected, short_filter, long_filter, out_weight, out_grad):
        _, count, chan = projected.shape
        long, groups = long_filter.shape
        model = out_weight.shape[1]
        scale = 1.0 / math.sqrt(n_ctx * count * (chan // groups))
        steps = dims[2] // 2
        anywhere = pl.BlockSpec(memory_space=pl.ANY)
        vmem = pl.BlockSpec(memory_space=pltpu.VMEM)
        dma = pltpu.SemaphoreType.DMA
        return pl.pallas_call(
            functools.partial(kernel, dims, scale),
            name="hyena_backward",
            out_shape=(
                jax.ShapeDtypeStruct(projected.shape, BF),
                jax.ShapeDtypeStruct(short_filter.shape, F32),
                jax.ShapeDtypeStruct(long_filter.shape, F32),
            ),
            in_specs=[anywhere, vmem, vmem, anywhere, anywhere],
            out_specs=(anywhere, vmem, vmem),
            scratch_shapes=[
                pltpu.VMEM((n_tp, out_grad.shape[0], model), BF),
                pltpu.VMEM((chan, model), BF),
                pltpu.VMEM((3, HALO + count, chan), BF),
                pltpu.VMEM((3, HALO + count, chan), F32),
                pltpu.VMEM((3, long + count, chan), BF),
                pltpu.VMEM((long + count, chan), BF),
                pltpu.VMEM((count, chan), F32),
                pltpu.VMEM((groups * long, 2 * long), BF),
                pltpu.VMEM((groups * long, 2 * long), BF),
                pltpu.VMEM((groups, 2 * long), F32),
                pltpu.VMEM((groups, 2 * long), F32),
                pltpu.VMEM((3, 8, chan), F32),
                pltpu.VMEM((count, chan), BF),
                pltpu.VMEM((count + 2 * long, chan), BF),
                pltpu.VMEM((long, chan), BF),
                pltpu.VMEM((3, long + count + 16, chan), F32),
                pltpu.VMEM((3, 16, chan), BF),
                pltpu.VMEM((3, 16, chan), BF),
                pltpu.VMEM((long, chan), F32),
                pltpu.VMEM((groups, 2 * long), F32),
                pltpu.VMEM((3, 8, chan), F32),
                pltpu.VMEM((dims[0], groups + 8, long), F32),
                pltpu.VMEM((dims[1], groups + 8, long), F32),
                pltpu.VMEM((3, count, chan), BF),
                dma((3,)),
                dma((2, steps, 2)),
                dma((2, steps, 2)),
                dma((2, steps + 1, 2)),
                dma((2, steps + 1, 2)),
                dma((3,)),
                dma((3,)),
                dma((max(1, dims[0] - 1),)),
                dma((dims[0],)),
                dma((max(1, dims[1] - 1),)),
                dma((dims[1],)),
                dma,
            ],
            compiler_params=pltpu.CompilerParams(
                collective_id=0, has_side_effects=True, vmem_limit_bytes=60 * 1024 * 1024
            ),
        )(projected, short_filter, long_filter, out_weight, out_grad)

    placed = (
        P(None, "ctx", "tp"),
        P(None, None, "tp"),
        P(None, "tp"),
        P("tp", None),
        P(("ctx", "tp"), None),
    )
    return jax.shard_map(
        step,
        mesh=mesh,
        in_specs=placed,
        out_specs=(P(None, "ctx", "tp"), P(None, None, "tp"), P(None, "tp")),
        check_vma=False,
    )
```

time: 564 us -> 85.5 us (0.15)
  the two profiles are of different devices: /device:TPU:112 before, /device:TPU:1 now
where the time goes in v1:
time: 85.5 us; the launch traced here: 85.1 us
  Pallas kernels  78.1 us (91%)
  local copies, waits for them, and re-layouts  6.3 us (7%)
    pallas_call x1, Pallas kernels, step(): pl.pallas_call(functools.partial(kernel, dims, scale), name='hyena_backwa...  78.1 us
    unnamed x3, local copies, waits for them, and re-layouts  4.78 us

profile of v1, /device:TPU:1, one launch (start us, length us, event | category | flops | bytes accessed | tf_op | source)
XLA Modules:
  0.0 85.1 jit_solution(10643401517210948607)
XLA Ops:
  0.6 1.4 %copy.8.lf_ref = bf16[128,32]{1,0:T(8,128)(2,1)} copy(bf16[128,32]{0,1:T(8,128)(2,1)} %param.7) | data formatting | bytes 16384 | tf_op args[2]
  2.0 78.1 %hyena_backward.1 = (bf16[3,256,512]{2,1,0:T(8,128)(2,1)}, f32[3,7,32]{2,1,0:T(8,128)}, f32[128,32]{1,0:T(8,128)}) custom-call(bf16[3,256,512]{2,1,0:T(8,128)(2,1)} %proj_hbm.1, f32[3,7,32]{2,1,0:T(8,128)} %sf_ref.1, bf16[128,32]{1,0:T(8,128)(2,1)} %copy.8.lf_ref, bf16[512,8192]{1,0:T(8,128)(2,1)} %w_hbm.1, bf16[16,8192]{1,0:T(8,128)(2,1)} %og_hbm.1), custom_call_target="tpu_custom_call" | custom-call | tf_op jit(solution)/shard_map/hyena_backward/pallas_call | solution.py:557
  80.2 1.5 %copy.9 = f32[128,32]{0,1:T(8,128)} copy(f32[128,32]{1,0:T(8,128)} %get-tuple-element.5) | data formatting | bytes 32768 | tf_op jit(solution)/shard_map/hyena_backward/pallas_call | solution.py:557
  81.7 2.1 %copy.12 = bf16[3,256,512]{2,1,0:T(8,128)(2,1)} copy(bf16[3,256,512]{2,1,0:T(8,128)(2,1)} %get-tuple-element.9) | data formatting | bytes 1572864
  83.8 1.3 %copy.13 = f32[3,7,32]{2,1,0:T(8,128)} copy(f32[3,7,32]{2,1,0:T(8,128)} %get-tuple-element.10) | data formatting | bytes 5376

commit v2 on v1

v2 whole, which is shorter than its diff:
```python
import functools
import math

import jax
import jax.numpy as jnp
from jax import lax
from jax.experimental import pallas as pl
from jax.experimental.pallas import tpu as pltpu
from jax.sharding import PartitionSpec as P

MESH = pl.DeviceIdType.MESH
BF = jnp.bfloat16
F32 = jnp.float32
HALO = 144
LB = 128
PIECES = 4
NT = (((1,), (1,)), ((), ()))
HI = lax.Precision.HIGHEST


def one_hot(shape, test):
    rows = lax.broadcasted_iota(jnp.int32, shape, 0)
    cols = lax.broadcasted_iota(jnp.int32, shape, 1)
    return jnp.where(test(rows, cols), 1.0, 0.0)


def kernel(
    dims,
    scale,
    proj_hbm,
    sf_ref,
    lf_ref,
    w_hbm,
    og_hbm,
    pg_hbm,
    sg_ref,
    lg_ref,
    gath,
    wv,
    pw,
    pf,
    mixed,
    prod,
    resp,
    fmat,
    bmat,
    taps_f,
    taps_b,
    taps_ch,
    acc,
    grb,
    nxt,
    gm,
    head_out,
    head_in,
    gp1,
    lacc,
    sgc,
    first_x,
    then_z,
    first_z,
    then_x,
    short_x,
    short_z,
    tmp,
    pgv,
    local_sem,
    ring_send,
    ring_recv,
    sib_send,
    sib_recv,
    halo_send,
    halo_recv,
    sum_send,
    sum_recv,
    out_sem,
):
    nx, nz, ny = dims
    n_ctx = nx * nz
    i = lax.axis_index("ctx")
    k = lax.axis_index("tp")
    x, z = lax.rem(i, nx), i // nx
    y, core = k // 2, lax.rem(k, 2)
    count = proj_hbm.shape[1]
    chan = proj_hbm.shape[2]
    model = w_hbm.shape[1]
    short = sf_ref.shape[1]
    groups, long = lf_ref.shape
    per_group = chan // groups
    lanes_n = chan // LB
    in_block = LB // per_group
    rows_chip = 2 * og_hbm.shape[0]
    piece = model // PIECES

    right = lax.rem(y + 1, ny) * 2 + core
    left = lax.rem(y + ny - 1, ny) * 2 + core
    sibling = y * 2 + 1 - core
    following = lax.rem(i + 1, n_ctx)
    previous = lax.rem(i + n_ctx - 1, n_ctx)
    x_peers = [z * nx + lax.rem(x + d, nx) for d in range(1, nx)]
    z_peers = [lax.rem(z + d, nz) * nx + x for d in range(1, nz)]

    barrier = pltpu.get_barrier_semaphore()
    tp_greet = [right, left, sibling]
    ctx_greet = [following, previous] + x_peers + z_peers
    for other in tp_greet:
        pl.semaphore_signal(barrier, inc=1, device_id={"tp": other}, device_id_type=MESH)
    for other in ctx_greet:
        pl.semaphore_signal(barrier, inc=1, device_id={"ctx": other}, device_id_type=MESH)

    og_copy = pltpu.make_async_copy(og_hbm, gath.at[k], local_sem.at[0])
    og_copy.start()
    proj_copy = pltpu.make_async_copy(proj_hbm, pw.at[:, pl.ds(HALO, count), :], local_sem.at[1])
    proj_copy.start()
    w_copy = pltpu.make_async_copy(w_hbm, wv, local_sem.at[2])
    w_copy.start()
    pl.semaphore_wait(barrier, len(tp_greet) + len(ctx_greet))

    steps = ny // 2

    def chunks(direction, step):
        if step < steps:
            return tuple(range(PIECES))
        return tuple(range(direction * PIECES // 2, (direction + 1) * PIECES // 2))

    def chip_at(direction, distance):
        if direction == 0:
            return lax.rem(y + ny - distance, ny)
        return lax.rem(y + distance, ny)

    def columns(chunk):
        return pl.ds(chunk * piece, piece)

    def ring(direction, step, chunk, arriving=False):
        block = chip_at(direction, step if arriving else step - 1) * 2 + core
        ref = gath.at[block, :, columns(chunk)]
        own = step == 1 and not arriving
        return pltpu.make_async_remote_copy(
            src_ref=og_hbm.at[:, columns(chunk)] if own else ref,
            dst_ref=ref,
            send_sem=ring_send.at[direction, step - 1, chunk],
            recv_sem=ring_recv.at[direction, step - 1, chunk],
            device_id={"tp": right if direction == 0 else left},
            device_id_type=MESH,
        )

    def across(direction, step, chunk, own):
        block = chip_at(direction, step) * 2 + (core if own else 1 - core)
        ref = gath.at[block, :, columns(chunk)]
        return pltpu.make_async_remote_copy(
            src_ref=og_hbm.at[:, columns(chunk)] if own and step == 0 else ref,
            dst_ref=ref,
            send_sem=sib_send.at[direction, step, chunk],
            recv_sem=sib_recv.at[direction, step, chunk],
            device_id={"tp": sibling},
            device_id_type=MESH,
        )

    for chunk in range(PIECES):
        for direction in range(2):
            if chunk in chunks(direction, 1):
                ring(direction, 1, chunk).start()
    halo = pltpu.make_async_remote_copy(
        src_ref=proj_hbm.at[:, pl.ds(count - HALO, HALO), :],
        dst_ref=pw.at[:, pl.ds(0, HALO), :],
        send_sem=halo_send.at[0],
        recv_sem=halo_recv.at[0],
        device_id={"ctx": following},
        device_id_type=MESH,
    )
    halo.start()
    for chunk in range(PIECES):
        across(0, 0, chunk, True).start()

    def service(step, which):
        for chunk in which:
            for direction in range(2):
                if chunk in chunks(direction, step):
                    ring(direction, step, chunk, True).wait_recv()
                    if step < steps and chunk in chunks(direction, step + 1):
                        ring(direction, step + 1, chunk).start()
                    across(direction, step, chunk, True).start()

    def across_arrivals(step, which=tuple(range(PIECES))):
        for direction in range(2 if step > 0 else 1):
            for chunk in chunks(direction, step):
                if chunk in which:
                    across(direction, step, chunk, False).wait_recv()

    def build_taps():
        spread = one_hot((groups, chan), lambda r, c: c // per_group == r)
        for j in range(3):
            taps_ch[j, 0:short, :] = jnp.dot(
                sf_ref[j], spread, precision=HI, preferred_element_type=F32
            )
        lf = lf_ref[...]
        backwards = one_hot((long, 2 * long), lambda r, c: c == long - r).astype(BF)
        taps_f[...] = jnp.dot(lf, backwards, preferred_element_type=F32)
        taps_b[:, 0:long] = lf.astype(F32)
        taps_b[:, long:] = jnp.zeros((groups, long), F32)

    def build_matrix(taps, matrix, start, stop):
        def body(g, carry):
            row = jnp.broadcast_to(taps[pl.ds(g, 1), :], (long, 2 * long))
            turned = pltpu.roll(row, 0, 1, stride=1, stride_axis=0)
            matrix[pl.ds(pl.multiple_of(g * long, long), long), :] = turned.astype(BF)
            return carry

        lax.fori_loop(start, stop, body, 0)

    lane_group = lax.broadcasted_iota(jnp.int32, (long, LB), 1) // per_group

    def pick(result, b):
        total = jnp.zeros((long, LB), F32)
        for g in range(in_block):
            piece = result[g * long : (g + 1) * long, b * LB : (b + 1) * LB]
            total = jnp.where(lane_group == g, piece, total)
        return total

    def lane_slice(lb):
        return pl.ds(pl.multiple_of(lb * LB, LB), LB)

    def group_rows(lb):
        return pl.ds(pl.multiple_of(lb * in_block * long, in_block * long), in_block * long)

    base = HALO - long
    far_rows = (long + count) // 8
    near_rows = count // 8

    def rows_apart(ref, j, lb, first, stride):
        return ref[j, lb, pl.ds(first, 8, stride=stride), :]

    def widen():
        def body(j, carry):
            for lb in range(lanes_n):
                ls = slice(lb * LB, (lb + 1) * LB)
                pf[j, lb, HALO : HALO + count, :] = pw[j, HALO : HALO + count, ls].astype(F32)
                edge = pw[j, 0:HALO, ls].astype(F32)
                pf[j, lb, 0:HALO, :] = jnp.where(i == 0, 0.0, edge)
            return carry

        lax.fori_loop(0, 3, body, 0)

    def short_forward():
        def body(step, carry):
            j, lb = step // lanes_n, lax.rem(step, lanes_n)
            ls = lane_slice(lb)
            taps = [jnp.broadcast_to(taps_ch[j, s : s + 1, ls], (8, LB)) for s in range(short)]
            held = [rows_apart(pf, j, lb, base - s, far_rows) for s in range(short - 1, 0, -1)]
            for q in range(far_rows):
                held.append(rows_apart(pf, j, lb, base + q, far_rows))
                total = taps[0] * held[-1]
                for s in range(1, short):
                    total = total + taps[s] * held[-1 - s]
                held = held[1:]
                mixed[j, lb, pl.ds(q, 8, stride=far_rows), :] = total.astype(BF).astype(F32)
            return carry

        lax.fori_loop(0, 3 * lanes_n, body, 0)

    def long_forward():
        def body(lb, carry):
            ls = lane_slice(lb)
            prod[:, ls] = (mixed[1, lb] * mixed[2, lb]).astype(BF)
            window = jnp.concatenate([prod[0 : 2 * long, ls], prod[long : 3 * long, ls]], axis=1)
            result = jnp.dot(fmat[group_rows(lb), :], window, preferred_element_type=F32)
            for b in range(2):
                resp[b * long : (b + 1) * long, ls] = pick(result, b)
            return carry

        lax.fori_loop(0, lanes_n, body, 0)

    kc = piece

    def project(chips, first=0, last=None):
        rows_n = rows_chip * len(chips)
        last = model // kc if last is None else last

        def body(c, carry):
            cols = pl.ds(pl.multiple_of(c * kc, kc), kc)
            xs = [gath[pl.ds(2 * chip, 2), :, cols].reshape(rows_chip, kc) for chip in chips]
            rhs = jnp.concatenate(xs, axis=0) if len(xs) > 1 else xs[0]
            return carry + lax.dot_general(wv[:, cols], rhs, NT, preferred_element_type=F32)

        total = jnp.zeros((chan, rows_n), F32)
        if last - first > 2:
            return lax.fori_loop(first, last, body, total)
        for c in range(first, last):
            total = body(c, total)
        return total

    def keep(total, chips):
        total = total.T.astype(BF)
        for q, chip in enumerate(chips):
            rows = pl.ds(pl.multiple_of(chip * rows_chip, rows_chip), rows_chip)
            acc[rows, :] = total[q * rows_chip : (q + 1) * rows_chip]

    def branch(chips):
        for chip in chips:
            start = chip * rows_chip
            rows = pl.ds(pl.multiple_of(start, rows_chip), rows_chip)
            own = pl.ds(pl.multiple_of(start + long, rows_chip), rows_chip)
            for lb in range(lanes_n):
                ls = slice(lb * LB, (lb + 1) * LB)
                ob = acc[rows, ls].astype(F32)
                gm[0, lb, own, :] = (ob * resp[rows, ls]).astype(BF).astype(F32)
                grb[own, ls] = (ob * mixed[0, lb, own, :]).astype(BF)

    low, high = tuple(range(PIECES // 2)), tuple(range(PIECES // 2, PIECES))
    build_taps()
    build_matrix(taps_f, fmat, 0, groups)
    grb[0:long, :] = jnp.zeros((long, chan), BF)
    grb[long + count :, :] = jnp.zeros((long, chan), BF)
    for j in range(3):
        sgc[j, :, :] = jnp.zeros((8, chan), F32)
    if steps > 1:
        service(1, low)
    build_matrix(taps_b, bmat, 0, groups * 3 // 4)
    if steps > 1:
        service(1, high)
    build_matrix(taps_b, bmat, groups * 3 // 4, groups)
    if steps > 2:
        service(2, low)
    proj_copy.wait()
    halo.wait_recv()
    widen()
    short_forward()
    if steps > 2:
        service(2, high)
    long_forward()
    near = [y]
    for step in range(1, steps - 1):
        near += [chip_at(0, step), chip_at(1, step)]
    og_copy.wait()
    w_copy.wait()
    for step in range(steps - 1):
        across_arrivals(step)
    if steps > 2:
        total = project(near, 0, PIECES // 2)
        service(3, low)
        keep(total + project(near, PIECES // 2, PIECES), near)
    else:
        keep(project(near), near)
    branch(near)
    if steps > 2:
        service(3, high)
    across_arrivals(steps - 1)
    far = [chip_at(0, steps - 1), chip_at(0, steps), chip_at(1, steps - 1)]
    total = jnp.zeros((chan, 3 * rows_chip), F32)
    for q in range(PIECES // 2):
        both = (q, q + PIECES // 2)
        service(steps, both)
        across_arrivals(steps, both)
        for chunk in both:
            total = total + project(far, chunk, chunk + 1)
    keep(total, far)
    branch(far)

    back = pltpu.make_async_remote_copy(
        src_ref=grb.at[pl.ds(long, long), :],
        dst_ref=nxt,
        send_sem=halo_send.at[1],
        recv_sem=halo_recv.at[1],
        device_id={"ctx": previous},
        device_id_type=MESH,
    )

    def set_products(rows, lb, grad):
        grad = grad.astype(BF).astype(F32)
        gm[1, lb, rows, :] = (grad * mixed[2, lb, rows, :]).astype(BF).astype(F32)
        gm[2, lb, rows, :] = (grad * mixed[1, lb, rows, :]).astype(BF).astype(F32)

    def long_backward(start, stop):
        def body(lb, carry):
            ls = lane_slice(lb)
            window = jnp.concatenate(
                [grb[b * long : (b + 2) * long, ls] for b in range(3)], axis=1
            )
            result = jnp.dot(bmat[group_rows(lb), :], window, preferred_element_type=F32)
            for b in range(3):
                grad = pick(result, b)
                if b == 2:
                    gp1[:, ls] = grad
                set_products(slice(b * long, (b + 1) * long), lb, grad)
            return carry

        lax.fori_loop(start, stop, body, 0)

    def long_taps():
        flip = one_hot((long, long), lambda r, c: r + c == long - 1).astype(BF)
        wide_group = lax.broadcasted_iota(jnp.int32, (long, 2 * LB), 1) % LB // per_group

        def body(lb, carry):
            ls = lane_slice(lb)
            grads = jnp.concatenate(
                [grb[long : 2 * long, ls], grb[2 * long : 3 * long, ls]], axis=1
            )
            grads = jnp.dot(flip, grads, preferred_element_type=F32).astype(BF)
            window = jnp.concatenate([prod[0 : 2 * long, ls], prod[long : 3 * long, ls]], axis=1)
            only = [
                jnp.where(wide_group == g, grads, jnp.zeros_like(grads)) for g in range(in_block)
            ]
            table = lax.dot_general(
                jnp.concatenate(only, axis=0), window, NT, preferred_element_type=F32
            )
            sums = []
            for g in range(in_block):
                piece = table[g * long : (g + 1) * long]
                turned = pltpu.roll(piece, 0, 1, stride=1, stride_axis=0)
                sums.append(jnp.sum(turned[:, long:], axis=0, keepdims=True))
            rows = pl.ds(pl.multiple_of(lb * in_block, in_block), in_block)
            lacc[rows, :] = jnp.concatenate(sums, axis=0)
            return carry

        lax.fori_loop(0, lanes_n, body, 0)

    def short_taps(streams, first, apart):
        def body(step, carry):
            j, lb = streams[0] + step // lanes_n, lax.rem(step, lanes_n)
            ls = lane_slice(lb)
            origin = base + first
            held = [rows_apart(pf, j, lb, origin - s, apart) for s in range(short - 1, 0, -1)]
            sums = [jnp.zeros((8, LB), F32)] * short
            for q in range(apart):
                held.append(rows_apart(pf, j, lb, origin + q, apart))
                grad = rows_apart(gm, j, lb, first + q, apart)
                sums = [sums[s] + grad * held[-1 - s] for s in range(short)]
                held = held[1:]
            for s in range(short):
                sgc[j, s : s + 1, ls] = jnp.sum(sums[s], axis=0, keepdims=True)
            return carry

        lax.fori_loop(0, len(streams) * lanes_n, body, 0)

    def exchange(number, buf, me, size, peers):
        def copy(slot, d):
            return pltpu.make_async_remote_copy(
                src_ref=buf.at[slot],
                dst_ref=buf.at[slot],
                send_sem=sum_send.at[number, d - 1],
                recv_sem=sum_recv.at[number, slot],
                device_id={"ctx": peers[d - 1]},
                device_id_type=MESH,
            )

        out = [copy(me, d) for d in range(1, size)]
        order = sorted(range(size - 1), key=lambda d: -min(d + 1, size - d - 1))
        return [out[d] for d in order], [copy(lax.rem(me + d, size), d) for d in range(1, size)]

    stage_ax = exchange(0, first_x, x, nx, x_peers)
    stage_az = exchange(1, then_z, z, nz, z_peers)
    stage_bz = exchange(2, first_z, z, nz, z_peers)
    stage_bx = exchange(3, then_x, x, nx, x_peers)
    stage_sx = exchange(4, short_x, x, nx, x_peers)
    stage_sz = exchange(5, short_z, z, nz, z_peers)

    def send(stage):
        for copy in stage[0]:
            copy.start()

    def gathered(stage, buf):
        for copy in stage[1]:
            copy.wait_recv()
        total = buf[0]
        for d in range(1, buf.shape[0]):
            total = total + buf[d]
        return total

    back.start()
    long_taps()
    part = groups // 2
    first_x[x, :, :] = lacc[0:part, :]
    first_z[z, :, :] = lacc[part:groups, :]
    long_backward(0, 1)
    send(stage_ax)
    send(stage_bz)
    long_backward(1, lanes_n)
    for lb in range(lanes_n):
        ls = slice(lb * LB, (lb + 1) * LB)
        head_out[:, :, ls] = gm[:, lb, long : long + 16, :].astype(BF)
    short_taps((1, 2), 0, far_rows)
    short_taps((0,), long, near_rows)
    head = pltpu.make_async_remote_copy(
        src_ref=head_out,
        dst_ref=head_in,
        send_sem=halo_send.at[2],
        recv_sem=halo_recv.at[2],
        device_id={"ctx": previous},
        device_id_type=MESH,
    )
    head.start()
    total = jnp.zeros((8, LB), F32)
    for j in range(3):
        place = one_hot((chan, LB), lambda r, c: c - groups * j == r // per_group)
        total = total + jnp.dot(sgc[j], place, precision=HI, preferred_element_type=F32)
    short_x[x, :, :] = total
    last = i == n_ctx - 1

    def finish_backward(start, stop):
        def body(lb, carry):
            ls = lane_slice(lb)
            window = nxt[:, ls]
            window = jnp.where(last, jnp.zeros_like(window), window)
            result = jnp.dot(
                bmat[group_rows(lb), long : 2 * long], window, preferred_element_type=F32
            )
            set_products(slice(2 * long, 3 * long), lb, gp1[:, ls] + pick(result, 0))
            return carry

        lax.fori_loop(start, stop, body, 0)

    back.wait_recv()
    finish_backward(0, 1)
    send(stage_sx)
    then_z[z, :, :] = gathered(stage_ax, first_x)
    then_x[x, :, :] = gathered(stage_bz, first_z)
    finish_backward(1, 2)
    send(stage_az)
    send(stage_bx)
    finish_backward(2, lanes_n)
    head.wait_recv()
    for lb in range(lanes_n):
        ls = slice(lb * LB, (lb + 1) * LB)
        ahead = jnp.where(last, 0.0, head_in[:, :, ls].astype(F32))
        gm[:, lb, long + count : long + count + 16, :] = ahead
    short_z[z, :, :] = gathered(stage_sx, short_x)

    def short_backward(start, stop):
        def body(step, carry):
            j, lb = step // lanes_n, lax.rem(step, lanes_n)
            ls = lane_slice(lb)
            taps = [jnp.broadcast_to(taps_ch[j, s : s + 1, ls], (8, LB)) for s in range(short)]
            held = [rows_apart(gm, j, lb, long + s, near_rows) for s in range(short - 1)]
            for q in range(near_rows):
                held.append(rows_apart(gm, j, lb, long + q + short - 1, near_rows))
                total = taps[0] * held[0]
                for s in range(1, short):
                    total = total + taps[s] * held[s]
                held = held[1:]
                tmp[j, lb, pl.ds(q, 8, stride=near_rows), :] = total
            pgv[j, :, ls] = tmp[j, lb].astype(BF)
            return carry

        lax.fori_loop(start, stop, body, 0)

    short_backward(0, lanes_n)
    send(stage_sz)
    short_backward(lanes_n, 3 * lanes_n)
    out_copy = pltpu.make_async_copy(pgv, pg_hbm, out_sem)
    out_copy.start()
    upper = gathered(stage_az, then_z)
    lower = gathered(stage_bx, then_x)
    total = jnp.concatenate([upper, lower], axis=0) * scale
    lg_ref[...] = jnp.dot(
        total,
        one_hot((long, long), lambda r, c: r + c == long - 1),
        precision=HI,
        preferred_element_type=F32,
    )
    total = gathered(stage_sz, short_z) * scale
    for j in range(3):
        place = one_hot((LB, groups), lambda r, c: r - groups * j == c)
        sums = jnp.dot(total, place, precision=HI, preferred_element_type=F32)
        sg_ref[j] = sums[0:short]

    for step in range(1, steps + 1):
        for direction in range(2):
            for chunk in chunks(direction, step):
                ring(direction, step, chunk).wait_send()
                across(direction, step, chunk, True).wait_send()
    for chunk in range(PIECES):
        across(0, 0, chunk, True).wait_send()
    halo.wait_send()
    back.wait_send()
    head.wait_send()
    for stage in (stage_ax, stage_az, stage_bz, stage_bx, stage_sx, stage_sz):
        for copy in stage[0]:
            copy.wait_send()
    out_copy.wait()


def solution(mesh):
    n_ctx, n_tp = mesh.shape["ctx"], mesh.shape["tp"]
    nx = math.isqrt(n_ctx)
    nx = nx if nx * nx == n_ctx else n_ctx
    dims = (nx, n_ctx // nx, n_tp // 2)

    def step(projected, short_filter, long_filter, out_weight, out_grad):
        _, count, chan = projected.shape
        long, groups = long_filter.shape
        lanes_n = chan // LB
        most = max(dims[0], dims[1])
        part = groups // 2
        model = out_weight.shape[1]
        scale = 1.0 / math.sqrt(n_ctx * count * (chan // groups))
        steps = dims[2] // 2
        anywhere = pl.BlockSpec(memory_space=pl.ANY)
        vmem = pl.BlockSpec(memory_space=pltpu.VMEM)
        dma = pltpu.SemaphoreType.DMA
        outs = pl.pallas_call(
            functools.partial(kernel, dims, scale),
            name="hyena_backward",
            out_shape=(
                jax.ShapeDtypeStruct(projected.shape, BF),
                jax.ShapeDtypeStruct(short_filter.shape, F32),
                jax.ShapeDtypeStruct((groups, long), F32),
            ),
            in_specs=[anywhere, vmem, vmem, anywhere, anywhere],
            out_specs=(anywhere, vmem, vmem),
            scratch_shapes=[
                pltpu.VMEM((n_tp, out_grad.shape[0], model), BF),
                pltpu.VMEM((chan, model), BF),
                pltpu.VMEM((3, HALO + count, chan), BF),
                pltpu.VMEM((3, lanes_n, HALO + count, LB), F32),
                pltpu.VMEM((3, lanes_n, long + count, LB), F32),
                pltpu.VMEM((long + count, chan), BF),
                pltpu.VMEM((count, chan), F32),
                pltpu.VMEM((groups * long, 2 * long), BF),
                pltpu.VMEM((groups * long, 2 * long), BF),
                pltpu.VMEM((groups, 2 * long), F32),
                pltpu.VMEM((groups, 2 * long), F32),
                pltpu.VMEM((3, 8, chan), F32),
                pltpu.VMEM((count, chan), BF),
                pltpu.VMEM((count + 2 * long, chan), BF),
                pltpu.VMEM((long, chan), BF),
                pltpu.VMEM((3, lanes_n, long + count + 16, LB), F32),
                pltpu.VMEM((3, 16, chan), BF),
                pltpu.VMEM((3, 16, chan), BF),
                pltpu.VMEM((long, chan), F32),
                pltpu.VMEM((groups, long), F32),
                pltpu.VMEM((3, 8, chan), F32),
                pltpu.VMEM((dims[0], part, long), F32),
                pltpu.VMEM((dims[1], part, long), F32),
                pltpu.VMEM((dims[1], part, long), F32),
                pltpu.VMEM((dims[0], part, long), F32),
                pltpu.VMEM((dims[0], 8, LB), F32),
                pltpu.VMEM((dims[1], 8, LB), F32),
                pltpu.VMEM((3, lanes_n, count, LB), F32),
                pltpu.VMEM((3, count, chan), BF),
                dma((3,)),
                dma((2, steps, PIECES)),
                dma((2, steps, PIECES)),
                dma((2, steps + 1, PIECES)),
                dma((2, steps + 1, PIECES)),
                dma((3,)),
                dma((3,)),
                dma((6, max(1, most - 1))),
                dma((6, most)),
                dma,
            ],
            compiler_params=pltpu.CompilerParams(
                collective_id=0, has_side_effects=True, vmem_limit_bytes=60 * 1024 * 1024
            ),
        )(projected, short_filter, long_filter.T, out_weight, out_grad)
        return outs[0], outs[1], outs[2].T

    placed = (
        P(None, "ctx", "tp"),
        P(None, None, "tp"),
        P(None, "tp"),
        P("tp", None),
        P(("ctx", "tp"), None),
    )
    return jax.shard_map(
        step,
        mesh=mesh,
        in_specs=placed,
        out_specs=(P(None, "ctx", "tp"), P(None, None, "tp"), P(None, "tp")),
        check_vma=False,
    )
```

time: 85.5 us -> 79.7 us (0.932)
  the two profiles are of different devices: /device:TPU:1 before, /device:TPU:32 now
where the time goes in v2:
time: 79.7 us; the launch traced here: 79.2 us
  Pallas kernels  73.9 us (93%)
  local copies, waits for them, and re-layouts  4.69 us (6%)
    pallas_call x1, Pallas kernels, step(): pl.pallas_call(functools.partial(kernel, dims, scale), name='hyena_backwa...  73.9 us
    unnamed x3, local copies, waits for them, and re-layouts  4.69 us

profile of v2, /device:TPU:32, one launch (start us, length us, event | category | flops | bytes accessed | tf_op | source)
XLA Modules:
  0.0 79.2 jit_solution(4446436571268447583)
XLA Ops:
  0.6 73.9 %hyena_backward.1 = (bf16[3,256,512]{2,1,0:T(8,128)(2,1)}, f32[3,7,32]{2,1,0:T(8,128)}, f32[32,128]{1,0:T(8,128)}) custom-call(bf16[3,256,512]{2,1,0:T(8,128)(2,1)} %proj_hbm.1, f32[3,7,32]{2,1,0:T(8,128)} %sf_ref.1, bf16[32,128]{1,0:T(8,128)(2,1)} %bitcast.3, bf16[512,8192]{1,0:T(8,128)(2,1)} %w_hbm.1, bf16[16,8192]{1,0:T(8,128)(2,1)} %og_hbm.1), custom_call_target="tpu_custom_call" | custom-call | tf_op jit(solution)/shard_map/hyena_backward/pallas_call | solution.py:600
  74.5 2.1 %copy.11 = bf16[3,256,512]{2,1,0:T(8,128)(2,1)} copy(bf16[3,256,512]{2,1,0:T(8,128)(2,1)} %get-tuple-element.12) | data formatting | bytes 1572864
  76.6 1.3 %copy.12 = f32[3,7,32]{2,1,0:T(8,128)} copy(f32[3,7,32]{2,1,0:T(8,128)} %get-tuple-element.13) | data formatting | bytes 5376
  77.9 1.3 %copy.13 = f32[128,32]{0,1:T(8,128)} copy(f32[128,32]{0,1:T(8,128)} %bitcast.2) | data formatting | bytes 32768

commit v3 on v2

--- a/solution.py
+++ b/solution.py
@@ -13,7 +13,7 @@
 F32 = jnp.float32
 HALO = 144
 LB = 128
-PIECES = 4
+PIECES = 8
 NT = (((1,), (1,)), ((), ()))
 HI = lax.Precision.HIGHEST
 
@@ -218,10 +218,11 @@
         return total
 
     def lane_slice(lb):
-        return pl.ds(pl.multiple_of(lb * LB, LB), LB)
+        return pl.ds(lb * LB if isinstance(lb, int) else pl.multiple_of(lb * LB, LB), LB)
 
     def group_rows(lb):
-        return pl.ds(pl.multiple_of(lb * in_block * long, in_block * long), in_block * long)
+        size = in_block * long
+        return pl.ds(lb * size if isinstance(lb, int) else pl.multiple_of(lb * size, size), size)
 
     base = HALO - long
     far_rows = (long + count) // 8
@@ -270,24 +271,19 @@
 
         lax.fori_loop(0, lanes_n, body, 0)
 
-    kc = piece
-
-    def project(chips, first=0, last=None):
-        rows_n = rows_chip * len(chips)
-        last = model // kc if last is None else last
-
+    kc = 2 * piece
+
+    def project(chips, first, size):
+        cols = pl.ds(first, size)
+        xs = [gath[pl.ds(2 * chip, 2), :, cols].reshape(rows_chip, size) for chip in chips]
+        rhs = jnp.concatenate(xs, axis=0) if len(xs) > 1 else xs[0]
+        return lax.dot_general(wv[:, cols], rhs, NT, preferred_element_type=F32)
+
+    def project_range(chips, first, last, total):
         def body(c, carry):
-            cols = pl.ds(pl.multiple_of(c * kc, kc), kc)
-            xs = [gath[pl.ds(2 * chip, 2), :, cols].reshape(rows_chip, kc) for chip in chips]
-            rhs = jnp.concatenate(xs, axis=0) if len(xs) > 1 else xs[0]
-            return carry + lax.dot_general(wv[:, cols], rhs, NT, preferred_element_type=F32)
-
-        total = jnp.zeros((chan, rows_n), F32)
-        if last - first > 2:
-            return lax.fori_loop(first, last, body, total)
-        for c in range(first, last):
-            total = body(c, total)
-        return total
+            return carry + project(chips, pl.multiple_of(c * kc, kc), kc)
+
+        return lax.fori_loop(first * piece // kc, last * piece // kc, body, total)
 
     def keep(total, chips):
         total = total.T.astype(BF)
@@ -321,12 +317,13 @@
     build_matrix(taps_b, bmat, groups * 3 // 4, groups)
     if steps > 2:
         service(2, low)
+        service(2, high)
     proj_copy.wait()
     halo.wait_recv()
     widen()
     short_forward()
     if steps > 2:
-        service(2, high)
+        service(3, low)
     long_forward()
     near = [y]
     for step in range(1, steps - 1):
@@ -335,24 +332,22 @@
     w_copy.wait()
     for step in range(steps - 1):
         across_arrivals(step)
-    if steps > 2:
-        total = project(near, 0, PIECES // 2)
-        service(3, low)
-        keep(total + project(near, PIECES // 2, PIECES), near)
-    else:
-        keep(project(near), near)
-    branch(near)
+    total = jnp.zeros((chan, len(near) * rows_chip), F32)
+    total = project_range(near, 0, PIECES // 2, total)
     if steps > 2:
         service(3, high)
-    across_arrivals(steps - 1)
+    total = project_range(near, PIECES // 2, PIECES, total)
+    keep(total, near)
+    branch(near)
     far = [chip_at(0, steps - 1), chip_at(0, steps), chip_at(1, steps - 1)]
     total = jnp.zeros((chan, 3 * rows_chip), F32)
+    across_arrivals(steps - 1)
     for q in range(PIECES // 2):
         both = (q, q + PIECES // 2)
         service(steps, both)
         across_arrivals(steps, both)
         for chunk in both:
-            total = total + project(far, chunk, chunk + 1)
+            total = total + project(far, chunk * piece, piece)
     keep(total, far)
     branch(far)
 
@@ -370,21 +365,28 @@
         gm[1, lb, rows, :] = (grad * mixed[2, lb, rows, :]).astype(BF).astype(F32)
         gm[2, lb, rows, :] = (grad * mixed[1, lb, rows, :]).astype(BF).astype(F32)
 
-    def long_backward(start, stop):
-        def body(lb, carry):
-            ls = lane_slice(lb)
-            window = jnp.concatenate(
-                [grb[b * long : (b + 2) * long, ls] for b in range(3)], axis=1
-            )
-            result = jnp.dot(bmat[group_rows(lb), :], window, preferred_element_type=F32)
-            for b in range(3):
-                grad = pick(result, b)
-                if b == 2:
-                    gp1[:, ls] = grad
-                set_products(slice(b * long, (b + 1) * long), lb, grad)
-            return carry
-
-        lax.fori_loop(start, stop, body, 0)
+    def long_backward(lb):
+        ls = lane_slice(lb)
+        window = jnp.concatenate([grb[b * long : (b + 2) * long, ls] for b in range(3)], axis=1)
+        result = jnp.dot(bmat[group_rows(lb), :], window, preferred_element_type=F32)
+        for b in range(3):
+            grad = pick(result, b)
+            if b == 2:
+                gp1[:, ls] = grad
+            set_products(slice(b * long, (b + 1) * long), lb, grad)
+
+    def short_taps(j, lb, first, apart):
+        ls = lane_slice(lb)
+        origin = base + first
+        held = [rows_apart(pf, j, lb, origin - s, apart) for s in range(short - 1, 0, -1)]
+        sums = [jnp.zeros((8, LB), F32)] * short
+        for q in range(apart):
+            held.append(rows_apart(pf, j, lb, origin + q, apart))
+            grad = rows_apart(gm, j, lb, first + q, apart)
+            sums = [sums[s] + grad * held[-1 - s] for s in range(short)]
+            held = held[1:]
+        for s in range(short):
+            sgc[j, s : s + 1, ls] = jnp.sum(sums[s], axis=0, keepdims=True)
 
     def long_taps():
         flip = one_hot((long, long), lambda r, c: r + c == long - 1).astype(BF)
@@ -410,27 +412,10 @@
                 sums.append(jnp.sum(turned[:, long:], axis=0, keepdims=True))
             rows = pl.ds(pl.multiple_of(lb * in_block, in_block), in_block)
             lacc[rows, :] = jnp.concatenate(sums, axis=0)
+            short_taps(0, lb, long, near_rows)
             return carry
 
         lax.fori_loop(0, lanes_n, body, 0)
-
-    def short_taps(streams, first, apart):
-        def body(step, carry):
-            j, lb = streams[0] + step // lanes_n, lax.rem(step, lanes_n)
-            ls = lane_slice(lb)
-            origin = base + first
-            held = [rows_apart(pf, j, lb, origin - s, apart) for s in range(short - 1, 0, -1)]
-            sums = [jnp.zeros((8, LB), F32)] * short
-            for q in range(apart):
-                held.append(rows_apart(pf, j, lb, origin + q, apart))
-                grad = rows_apart(gm, j, lb, first + q, apart)
-                sums = [sums[s] + grad * held[-1 - s] for s in range(short)]
-                held = held[1:]
-            for s in range(short):
-                sgc[j, s : s + 1, ls] = jnp.sum(sums[s], axis=0, keepdims=True)
-            return carry
-
-        lax.fori_loop(0, len(streams) * lanes_n, body, 0)
 
     def exchange(number, buf, me, size, peers):
         def copy(slot, d):
@@ -466,20 +451,29 @@
             total = total + buf[d]
         return total
 
+    def backward_and_taps():
+        def body(lb, carry):
+            long_backward(lb)
+            short_taps(1, lb - 1, 0, far_rows)
+            short_taps(2, lb - 1, 0, far_rows)
+            return carry
+
+        lax.fori_loop(1, lanes_n, body, 0)
+        short_taps(1, lanes_n - 1, 0, far_rows)
+        short_taps(2, lanes_n - 1, 0, far_rows)
+
     back.start()
     long_taps()
     part = groups // 2
     first_x[x, :, :] = lacc[0:part, :]
     first_z[z, :, :] = lacc[part:groups, :]
-    long_backward(0, 1)
+    long_backward(0)
     send(stage_ax)
     send(stage_bz)
-    long_backward(1, lanes_n)
+    backward_and_taps()
     for lb in range(lanes_n):
         ls = slice(lb * LB, (lb + 1) * LB)
         head_out[:, :, ls] = gm[:, lb, long : long + 16, :].astype(BF)
-    short_taps((1, 2), 0, far_rows)
-    short_taps((0,), long, near_rows)
     head = pltpu.make_async_remote_copy(
         src_ref=head_out,
         dst_ref=head_in,
@@ -577,6 +571,21 @@
         for copy in stage[0]:
             copy.wait_send()
     out_copy.wait()
+
+
+def hand_over(pg_in, sg_in, lg_in, pg_out, sg_out, lg_out, pg, sg, lg, sem_in, sem_out):
+    moves = [(sg_in, sg, sg_out), (lg_in, lg, lg_out)]
+    for j in range(3):
+        moves.append((pg_in.at[j], pg.at[j], pg_out.at[j]))
+    loads = [pltpu.make_async_copy(m[0], m[1], sem_in.at[n]) for n, m in enumerate(moves)]
+    stores = [pltpu.make_async_copy(m[1], m[2], sem_out.at[n]) for n, m in enumerate(moves)]
+    for copy in loads:
+        copy.start()
+    for load, store in zip(loads, stores):
+        load.wait()
+        store.start()
+    for copy in stores:
+        copy.wait()
 
 
 def solution(mesh):
@@ -652,6 +661,14 @@
                 collective_id=0, has_side_effects=True, vmem_limit_bytes=60 * 1024 * 1024
             ),
         )(projected, short_filter, long_filter.T, out_weight, out_grad)
+        outs = pl.pallas_call(
+            hand_over,
+            name="hand_over",
+            out_shape=tuple(jax.ShapeDtypeStruct(o.shape, o.dtype) for o in outs),
+            in_specs=[anywhere] * 3,
+            out_specs=(anywhere,) * 3,
+            scratch_shapes=[pltpu.VMEM(o.shape, o.dtype) for o in outs] + [dma((5,)), dma((5,))],
+        )(*outs)
         return outs[0], outs[1], outs[2].T
 
     placed = (

time: 79.7 us -> 78.1 us (0.980)
  local copies, waits for them, and re-layouts: 4.69 us -> 0 us
  Pallas kernels: 73.9 us -> 77.2 us
    unnamed x3 -> x0, local copies, waits for them, and re-layouts: 4.69 us -> none
    pallas_call x0 -> x1, Pallas kernels: none -> 1.95 us  [step(): pl.pallas_call(hand_over, name='hand_over', out_shape=tuple((jax.ShapeDty...]
    pallas_call x1, Pallas kernels: 73.9 us -> 75.2 us  [step(): pl.pallas_call(functools.partial(kernel, dims, scale), name='hyena_backwa...]
where the time goes in v3:
time: 78.1 us; the launch traced here: 77.8 us
  Pallas kernels  77.2 us (99%)
    pallas_call x1, Pallas kernels, step(): pl.pallas_call(functools.partial(kernel, dims, scale), name='hyena_backwa...  75.2 us
    pallas_call x1, Pallas kernels, step(): pl.pallas_call(hand_over, name='hand_over', out_shape=tuple((jax.ShapeDty...  1.95 us

profile of v3, /device:TPU:32, one launch (start us, length us, event | category | flops | bytes accessed | tf_op | source)
XLA Modules:
  0.0 77.8 jit_solution(6920783220757752217)
XLA Ops:
  0.6 75.2 %hyena_backward.1 = (bf16[3,256,512]{2,1,0:T(8,128)(2,1)}, f32[3,7,32]{2,1,0:T(8,128)}, f32[32,128]{1,0:T(8,128)}) custom-call(bf16[3,256,512]{2,1,0:T(8,128)(2,1)} %proj_hbm.1, f32[3,7,32]{2,1,0:T(8,128)} %sf_ref.1, bf16[32,128]{1,0:T(8,128)(2,1)} %bitcast.2, bf16[512,8192]{1,0:T(8,128)(2,1)} %w_hbm.1, bf16[16,8192]{1,0:T(8,128)(2,1)} %og_hbm.1), custom_call_target="tpu_custom_call" | custom-call | tf_op jit(solution)/shard_map/hyena_backward/pallas_call | solution.py:609
  75.8 1.9 %hand_over.1 = (bf16[3,256,512]{2,1,0:T(8,128)(2,1)}, f32[3,7,32]{2,1,0:T(8,128)}, f32[32,128]{1,0:T(8,128)}) custom-call(bf16[3,256,512]{2,1,0:T(8,128)(2,1)} %get-tuple-element.9.pg_in, f32[3,7,32]{2,1,0:T(8,128)} %get-tuple-element.10.sg_in, f32[32,128]{1,0:T(8,128)} %get-tuple-element.11.lg_in), custom_call_target="tpu_custom_call" | custom-call | tf_op jit(solution)/shard_map/hand_over/pallas_call | solution.py:664

commit v4 on v3

--- a/solution.py
+++ b/solution.py
@@ -13,7 +13,7 @@
 F32 = jnp.float32
 HALO = 144
 LB = 128
-PIECES = 8
+PIECES = 4
 NT = (((1,), (1,)), ((), ()))
 HI = lax.Precision.HIGHEST
 
@@ -271,7 +271,7 @@
 
         lax.fori_loop(0, lanes_n, body, 0)
 
-    kc = 2 * piece
+    kc = piece
 
     def project(chips, first, size):
         cols = pl.ds(first, size)
@@ -482,7 +482,6 @@
         device_id={"ctx": previous},
         device_id_type=MESH,
     )
-    head.start()
     total = jnp.zeros((8, LB), F32)
     for j in range(3):
         place = one_hot((chan, LB), lambda r, c: c - groups * j == r // per_group)
@@ -506,18 +505,21 @@
     back.wait_recv()
     finish_backward(0, 1)
     send(stage_sx)
+    head.start()
     then_z[z, :, :] = gathered(stage_ax, first_x)
     then_x[x, :, :] = gathered(stage_bz, first_z)
     finish_backward(1, 2)
     send(stage_az)
     send(stage_bx)
-    finish_backward(2, lanes_n)
+    finish_backward(2, lanes_n - 1)
+    short_z[z, :, :] = gathered(stage_sx, short_x)
+    finish_backward(lanes_n - 1, lanes_n)
+    send(stage_sz)
     head.wait_recv()
     for lb in range(lanes_n):
         ls = slice(lb * LB, (lb + 1) * LB)
         ahead = jnp.where(last, 0.0, head_in[:, :, ls].astype(F32))
         gm[:, lb, long + count : long + count + 16, :] = ahead
-    short_z[z, :, :] = gathered(stage_sx, short_x)
 
     def short_backward(start, stop):
         def body(step, carry):
@@ -537,9 +539,7 @@
 
         lax.fori_loop(start, stop, body, 0)
 
-    short_backward(0, lanes_n)
-    send(stage_sz)
-    short_backward(lanes_n, 3 * lanes_n)
+    short_backward(0, 3 * lanes_n)
     out_copy = pltpu.make_async_copy(pgv, pg_hbm, out_sem)
     out_copy.start()
     upper = gathered(stage_az, then_z)

time: 78.1 us -> 74.7 us (0.956)
  Pallas kernels: 77.2 us -> 73.8 us
    pallas_call x1, Pallas kernels: 75.2 us -> 71.8 us  [step(): pl.pallas_call(functools.partial(kernel, dims, scale), name='hyena_backwa...]
where the time goes in v4:
time: 74.7 us; the launch traced here: 74.4 us
  Pallas kernels  73.8 us (99%)
    pallas_call x1, Pallas kernels, step(): pl.pallas_call(functools.partial(kernel, dims, scale), name='hyena_backwa...  71.8 us
    pallas_call x1, Pallas kernels, step(): pl.pallas_call(hand_over, name='hand_over', out_shape=tuple((jax.ShapeDty...  1.95 us

profile of v4, /device:TPU:32, one launch (start us, length us, event | category | flops | bytes accessed | tf_op | source)
XLA Modules:
  0.0 74.4 jit_solution(1223357421218559606)
XLA Ops:
  0.6 71.8 %hyena_backward.1 = (bf16[3,256,512]{2,1,0:T(8,128)(2,1)}, f32[3,7,32]{2,1,0:T(8,128)}, f32[32,128]{1,0:T(8,128)}) custom-call(bf16[3,256,512]{2,1,0:T(8,128)(2,1)} %proj_hbm.1, f32[3,7,32]{2,1,0:T(8,128)} %sf_ref.1, bf16[32,128]{1,0:T(8,128)(2,1)} %bitcast.2, bf16[512,8192]{1,0:T(8,128)(2,1)} %w_hbm.1, bf16[16,8192]{1,0:T(8,128)(2,1)} %og_hbm.1), custom_call_target="tpu_custom_call" | custom-call | tf_op jit(solution)/shard_map/hyena_backward/pallas_call | solution.py:609
  72.5 1.9 %hand_over.1 = (bf16[3,256,512]{2,1,0:T(8,128)(2,1)}, f32[3,7,32]{2,1,0:T(8,128)}, f32[32,128]{1,0:T(8,128)}) custom-call(bf16[3,256,512]{2,1,0:T(8,128)(2,1)} %get-tuple-element.9.pg_in, f32[3,7,32]{2,1,0:T(8,128)} %get-tuple-element.10.sg_in, f32[32,128]{1,0:T(8,128)} %get-tuple-element.11.lg_in), custom_call_target="tpu_custom_call" | custom-call | tf_op jit(solution)/shard_map/hand_over/pallas_call | solution.py:664

commit v5 on v4

--- a/solution.py
+++ b/solution.py
@@ -446,9 +446,9 @@
     def gathered(stage, buf):
         for copy in stage[1]:
             copy.wait_recv()
-        total = buf[0]
+        total = buf[0].astype(F32)
         for d in range(1, buf.shape[0]):
-            total = total + buf[d]
+            total = total + buf[d].astype(F32)
         return total
 
     def backward_and_taps():
@@ -465,8 +465,8 @@
     back.start()
     long_taps()
     part = groups // 2
-    first_x[x, :, :] = lacc[0:part, :]
-    first_z[z, :, :] = lacc[part:groups, :]
+    first_x[x, :, :] = lacc[0:part, :].astype(BF)
+    first_z[z, :, :] = lacc[part:groups, :].astype(BF)
     long_backward(0)
     send(stage_ax)
     send(stage_bz)
@@ -506,8 +506,8 @@
     finish_backward(0, 1)
     send(stage_sx)
     head.start()
-    then_z[z, :, :] = gathered(stage_ax, first_x)
-    then_x[x, :, :] = gathered(stage_bz, first_z)
+    then_z[z, :, :] = gathered(stage_ax, first_x).astype(BF)
+    then_x[x, :, :] = gathered(stage_bz, first_z).astype(BF)
     finish_backward(1, 2)
     send(stage_az)
     send(stage_bx)
@@ -638,10 +638,10 @@
                 pltpu.VMEM((long, chan), F32),
                 pltpu.VMEM((groups, long), F32),
                 pltpu.VMEM((3, 8, chan), F32),
-                pltpu.VMEM((dims[0], part, long), F32),
-                pltpu.VMEM((dims[1], part, long), F32),
-                pltpu.VMEM((dims[1], part, long), F32),
-                pltpu.VMEM((dims[0], part, long), F32),
+                pltpu.VMEM((dims[0], part, long), BF),
+                pltpu.VMEM((dims[1], part, long), BF),
+                pltpu.VMEM((dims[1], part, long), BF),
+                pltpu.VMEM((dims[0], part, long), BF),
                 pltpu.VMEM((dims[0], 8, LB), F32),
                 pltpu.VMEM((dims[1], 8, LB), F32),
                 pltpu.VMEM((3, lanes_n, count, LB), F32),

time: 74.7 us -> 74.5 us (level)
  no operation moved by 1% of the time
where the time goes in v5:
time: 74.5 us; the launch traced here: 74.2 us
  Pallas kernels  73.6 us (99%)
    pallas_call x1, Pallas kernels, step(): pl.pallas_call(functools.partial(kernel, dims, scale), name='hyena_backwa...  71.6 us
    pallas_call x1, Pallas kernels, step(): pl.pallas_call(hand_over, name='hand_over', out_shape=tuple((jax.ShapeDty...  1.95 us

profile of v5, /device:TPU:32, one launch (start us, length us, event | category | flops | bytes accessed | tf_op | source)
XLA Modules:
  0.0 74.2 jit_solution(5346551608206631994)
XLA Ops:
  0.6 71.6 %hyena_backward.1 = (bf16[3,256,512]{2,1,0:T(8,128)(2,1)}, f32[3,7,32]{2,1,0:T(8,128)}, f32[32,128]{1,0:T(8,128)}) custom-call(bf16[3,256,512]{2,1,0:T(8,128)(2,1)} %proj_hbm.1, f32[3,7,32]{2,1,0:T(8,128)} %sf_ref.1, bf16[32,128]{1,0:T(8,128)(2,1)} %bitcast.2, bf16[512,8192]{1,0:T(8,128)(2,1)} %w_hbm.1, bf16[16,8192]{1,0:T(8,128)(2,1)} %og_hbm.1), custom_call_target="tpu_custom_call" | custom-call | tf_op jit(solution)/shard_map/hyena_backward/pallas_call | solution.py:609
  72.2 1.9 %hand_over.1 = (bf16[3,256,512]{2,1,0:T(8,128)(2,1)}, f32[3,7,32]{2,1,0:T(8,128)}, f32[32,128]{1,0:T(8,128)}) custom-call(bf16[3,256,512]{2,1,0:T(8,128)(2,1)} %get-tuple-element.9.pg_in, f32[3,7,32]{2,1,0:T(8,128)} %get-tuple-element.10.sg_in, f32[32,128]{1,0:T(8,128)} %get-tuple-element.11.lg_in), custom_call_target="tpu_custom_call" | custom-call | tf_op jit(solution)/shard_map/hand_over/pallas_call | solution.py:664
